TPU v7x, 1024 devices: a whole 4x8x16 slice. The times are simulated.
1024 devices in a mesh: pair: 2 (over y_lo), section: 16 (over z), dp: 32 (over y_hi, x, core).
Axes of the slice: x: 4, y: 8 (y_hi: 4, y_lo: 2; y = y_hi * 2 + y_lo), z: 16, core: 2. Of those that a mesh axis runs over, the one named last changes fastest.
Arguments:
- grads: float32 [32, 32, 64, 7168], P(('section', 'pair'), 'dp'), parts along dimension 0, may hold values from -6 to 6
- master: float32 [1024, 7168], P(('section', 'pair', 'dp')), parts along dimension 0, may hold values from -6 to 6
- moment: float32 [1024, 7168], P(('section', 'pair', 'dp')), parts along dimension 0, may hold values from -12 to 12
- second: float32 [1024, 7168], P(('section', 'pair', 'dp')), parts along dimension 0, may hold values from 0.5 to 50
- step: int32 [16], P('section'), parts along dimension 0, may hold values from 1 to 8
Outputs:
- new_master: float32 [1024, 7168], P(('section', 'pair', 'dp')), parts along dimension 0
- new_moment: float32 [1024, 7168], P(('section', 'pair', 'dp')), parts along dimension 0
- new_second: float32 [1024, 7168], P(('section', 'pair', 'dp')), parts along dimension 0
- params: bfloat16 [1024, 7168], P('section'), parts along dimension 0
There are 16 independent parts, one for each index of `section`. A program takes and returns all parts, laid end to end along the dimension named above; each array names one. Nothing has to cross between parts.
All inputs are finite; a program needn't handle non-finite values.
Results may differ from a plain program's by a relative error of at most 0.0004.
Values may be sent and summed in bfloat16 or wider, within the bound.
A program may use at most 32 MiB of HBM per device.

v0:
```python
import jax
import jax.numpy as jnp
from jax import lax
from jax.sharding import PartitionSpec as P


def per_device(grads, master, moment, second, step):
    local = grads.reshape(grads.shape[2], grads.shape[3])
    total = lax.psum_scatter(local, ("pair", "dp"), scatter_dimension=0, tiled=True)
    new_moment = 0.9 * moment + 0.1 * total
    new_second = 0.95 * second + 0.05 * total * total
    count = step[0].astype(jnp.float32)
    first_fix = 1.0 - jnp.power(jnp.float32(0.9), count)
    second_fix = 1.0 - jnp.power(jnp.float32(0.95), count)
    update = new_moment / first_fix / (jnp.sqrt(new_second / second_fix) + 1e-08) + 0.1 * master
    new_master = master - 0.03 * update
    shard_params = new_master.astype(jnp.bfloat16)
    params = lax.all_gather(shard_params, ("pair", "dp"), axis=0, tiled=True)
    return (new_master, new_moment, new_second, params)


def solution(mesh):
    placed = (
        P(("section", "pair"), "dp", None, None),
        P(("section", "pair", "dp"), None),
        P(("section", "pair", "dp"), None),
        P(("section", "pair", "dp"), None),
        P("section"),
    )
    return jax.shard_map(
        per_device,
        mesh=mesh,
        in_specs=placed,
        out_specs=(
            P(("section", "pair", "dp"), None),
            P(("section", "pair", "dp"), None),
            P(("section", "pair", "dp"), None),
            P("section", None),
        ),
        check_vma=False,
    )
```

profile of v0, /device:TPU:9, one launch (start us, length us, event | category | flops | bytes accessed | tf_op | source)
XLA Modules:
  0.0 342.1 jit_solution(14961512763501092211)
XLA Ops:
  7.2 0.0 copy-start
  7.2 0.0 copy-start.2
  7.2 0.0 copy-start.1
  7.2 0.0 all-reduce.3.cloned.1.call-start
  7.2 0.7 all-reduce.3.cloned.1.call-update
  8.7 1.3 dynamic-slice
  9.9 229.3 %all-reduce.3.cloned.1.call-done = f32[64,7168]{1,0:T(8,128)} async-done(((f32[64,7168]{1,0:T(8,128)}), f32[64,7168]{1,0:T(8,128)}) %all-reduce.3.cloned.1.call-update) | async-done | bytes 1835024
  239.2 0.0 copy-done
  239.2 0.0 copy-done.2
  239.2 0.0 copy-done.1
  239.2 2.4 convert_bitcast_fusion
  241.6 92.4 %all-gather = bf16[64,1,7168]{2,1,0:T(2,128)(2,1)S(1)} all-gather(bf16[1,1,7168]{2,1,0:T(2,128)(2,1)S(1)} %get-tuple-element.4), channel_id=1, replica_groups=mesh['pair'=2,'section'=16,'dp'=32] {'pair','dp'}, dimensions={0}, use_global_device_ids=true | all-gather | bytes 931840 | tf_op jit(solution)/shard_map/all_gather | solution.py:18
  334.0 1.2 copy.11
Async XLA Ops:
  7.2 232.0 %copy-start = (f32[1,7168]{1,0:T(1,128)S(1)}, f32[1,7168]{1,0:T(1,128)}, u32[]{:S(2)}) copy-start(f32[1,7168]{1,0:T(1,128)} %param.6) | copy-start | bytes 86020
  7.2 232.0 %copy-start.2 = (f32[1,7168]{1,0:T(1,128)S(1)}, f32[1,7168]{1,0:T(1,128)}, u32[]{:S(2)}) copy-start(f32[1,7168]{1,0:T(1,128)} %param.7) | copy-start | bytes 86020
  7.2 232.0 %copy-start.1 = (f32[1,7168]{1,0:T(1,128)S(1)}, f32[1,7168]{1,0:T(1,128)}, u32[]{:S(2)}) copy-start(f32[1,7168]{1,0:T(1,128)} %param.8) | copy-start | bytes 86020
  7.2 232.0 %all-reduce.3.cloned.1.call-start = ((), (), s32[]{:S(2)}) async-start(), calls=%async_computation | async-start | bytes 3670016
Sparse Core Ops, SparseCore 0:
  11.5 227.6 all-reduce.2
where the time goes:
time: 342 us
  waiting for transfers between devices  230 us (67%)
  blocking collectives  92.4 us (27%)
  between operations  14.8 us (4%)
    unnamed x2, waiting for transfers between devices  230 us
    all_gather x1, blocking collectives, per_device(): params = lax.all_gather(shard_params, ('pair', 'dp'), axis=0, tiled=True)  92.4 us
  transfers between devices with their start and end apart: 1, of which 1 were waited for; matrix products, arithmetic and copies ran while one was open for 0% of the time, Pallas kernels for 0%

commit v1 on v0

v1 whole, which is shorter than its diff:
```python
import functools

import jax
import jax.numpy as jnp
from jax import lax
from jax.experimental import pallas as pl
from jax.experimental.pallas import tpu as pltpu
from jax.sharding import PartitionSpec as P

MESH = pl.DeviceIdType.MESH
F32 = jnp.float32
BF16 = jnp.bfloat16
J = 56


def kernel(
    step_ref, g_ref, master_ref, moment_ref, second_ref,
    new_master_ref, new_moment_ref, new_second_ref, params_ref,
    mine, sib, xs, t3, t4, rm1, rm2, r3, r4, ys, yr, rows, wide,
    load_sem, d_send, d_recv, x_send, x_recv, y_send, y_recv,
    ay_send, a_recv, ax_send, ad_send,
):
    ylo = lax.axis_index("pair")
    dp = lax.axis_index("dp")
    c = lax.rem(dp, 2)
    x = lax.rem(dp // 2, 4)
    yhi = dp // 8
    y = yhi * 2 + ylo
    oc = 1 - c
    xp = lax.rem(x + 1, 4)
    xm = lax.rem(x + 3, 4)
    xo = lax.rem(x + 2, 4)

    def dev(lo, hi, xx, cc):
        return {"pair": lo, "dp": (hi * 4 + xx) * 2 + cc}

    sibling = dev(ylo, yhi, x, oc)
    plus = dev(ylo, yhi, xp, c)
    minus = dev(ylo, yhi, xm, c)

    def remote(src, dst, ssem, rsem, where):
        return pltpu.make_async_remote_copy(
            src_ref=src, dst_ref=dst, send_sem=ssem, recv_sem=rsem,
            device_id=where, device_id_type=MESH,
        )

    hi_of = [lax.rem(yhi + 2 + k, 4) for k in range(4)]

    loads = []
    for k in range(4):
        cp = pltpu.make_async_copy(g_ref.at[c * 4 + hi_of[k]], mine.at[k], load_sem.at[k])
        cp.start()
        loads.append(cp)

    barrier = pltpu.get_barrier_semaphore()
    for where in (sibling, plus, minus):
        pl.semaphore_signal(barrier, inc=1, device_id=where, device_id_type=MESH)
    for d in range(1, 8):
        yy = lax.rem(y + d, 8)
        for cc in range(2):
            pl.semaphore_signal(
                barrier, inc=1, device_id=dev(lax.rem(yy, 2), yy // 2, x, cc), device_id_type=MESH
            )
    pl.semaphore_wait(barrier, 17)

    d_copies = []
    for k in range(4):
        cp = remote(g_ref.at[oc * 4 + hi_of[k]], sib.at[k], d_send.at[k], d_recv.at[k], sibling)
        cp.start()
        d_copies.append(cp)

    pending = []

    def send(*args):
        cp = remote(*args)
        cp.start()
        pending.append(cp)
        return cp

    m1, m2, m3, m4 = {}, {}, {}, {}

    def stage_sum(k):
        loads[k].wait()
        d_copies[k].wait_recv()
        a = mine.at[k].reshape(J * 8, 128)
        b = sib.at[k].reshape(J * 8, 128)
        for s in range(8):
            for jb in range(7):
                sl = pl.ds(jb * 64 + s, 8, stride=8)
                xs[s // 2, k, s % 2, pl.ds(jb * 8, 8), :] = a[sl, :] + b[sl, :]
        m1[k] = send(xs.at[xo, k, 0], rm1.at[k], x_send.at[0, k], x_recv.at[0, k], plus)
        m2[k] = send(xs.at[xo, k, 1], rm2.at[k], x_send.at[1, k], x_recv.at[1, k], minus)
        m3[k, 1] = send(xs.at[xp, k, 1], r3.at[k, 1], x_send.at[2, k], x_recv.at[2, k], plus)
        m4[k, 0] = send(xs.at[xm, k, 0], r4.at[k, 0], x_send.at[3, k], x_recv.at[3, k], minus)

    def stage_relay(k):
        m1[k].wait_recv()
        t3[k] = xs[xp, k, 0] + rm1[k]
        m3[k, 0] = send(t3.at[k], r3.at[k, 0], x_send.at[4, k], x_recv.at[4, k], plus)
        m2[k].wait_recv()
        t4[k] = xs[xm, k, 1] + rm2[k]
        m4[k, 1] = send(t4.at[k], r4.at[k, 1], x_send.at[5, k], x_recv.at[5, k], minus)

    def stage_y(k):
        hi = hi_of[k]
        for cc in range(2):
            m3[k, cc].wait_recv()
            m4[k, cc].wait_recv()
            ys[k, cc] = xs[x, k, cc] + r3[k, cc] + r4[k, cc]
            if k == 2:
                own = jnp.logical_and(c == ylo, c == cc)

                @pl.when(own)
                def _():
                    yr[y] = ys[k, cc]

                @pl.when(jnp.logical_not(own))
                def _():
                    remote(ys.at[k, cc], yr.at[y], y_send.at[k, cc], y_recv.at[y], dev(c, hi, x, cc)).start()
            else:
                remote(ys.at[k, cc], yr.at[y], y_send.at[k, cc], y_recv.at[y], dev(c, hi, x, cc)).start()

    stage_sum(0)
    stage_sum(1)
    stage_relay(0)
    stage_sum(2)
    stage_relay(1)
    stage_sum(3)
    stage_relay(2)
    stage_y(0)
    stage_relay(3)
    stage_y(1)
    stage_y(2)
    stage_y(3)

    def y_wait(slot):
        remote(ys.at[0, 0], yr.at[slot], y_send.at[0, 0], y_recv.at[slot], sibling).wait_recv()

    @pl.when(c != ylo)
    def _():
        y_wait(y)

    for d in (1, 7, 2, 6, 3, 5, 4):
        y_wait(lax.rem(y + d, 8))
    total = yr[0]
    for i in range(1, 8):
        total = total + yr[i]

    t = step_ref[0]
    p1 = jnp.float32(1.0)
    p2 = jnp.float32(1.0)
    b1, b2 = 0.9, 0.95
    for bit in range(8):
        on = lax.rem(lax.shift_right_logical(t, bit), 2) == 1
        p1 = p1 * jnp.where(on, jnp.float32(b1), jnp.float32(1.0))
        p2 = p2 * jnp.where(on, jnp.float32(b2), jnp.float32(1.0))
        b1, b2 = b1 * b1, b2 * b2
    first_fix = 1.0 - p1
    second_fix = 1.0 - p2
    master = master_ref[...]
    new_moment = 0.9 * moment_ref[...] + 0.1 * total
    new_second = 0.95 * second_ref[...] + 0.05 * total * total
    ff = jnp.full((J, 128), first_fix, F32)
    sf = jnp.full((J, 128), second_fix, F32)
    update = new_moment / ff / (jnp.sqrt(new_second / sf) + 1e-08) + 0.1 * master
    new_master = master - 0.03 * update
    new_master_ref[...] = new_master
    new_moment_ref[...] = new_moment
    new_second_ref[...] = new_second

    def row_of(yy, xx, cc):
        return lax.rem(yy, 2) * 32 + (yy // 2) * 8 + xx * 2 + cc

    rows[row_of(y, x, c)] = new_master.astype(BF16)

    def pass_on(r, sems, where):
        send(rows.at[r], rows.at[r], sems, a_recv.at[r], where)

    def arrive(r):
        remote(rows.at[r], rows.at[r], ad_send.at[0], a_recv.at[r], sibling).wait_recv()

    me = row_of(y, x, c)
    for i, d in enumerate((4, 3, 5, 2, 6, 1, 7)):
        yy = lax.rem(y + d, 8)
        pass_on(me, ay_send.at[i], dev(lax.rem(yy, 2), yy // 2, x, c))
    far = (0, 1, 7, 2, 6, 3, 5, 4)

    def spread(i):
        yy = lax.rem(y + far[i], 8)
        r = row_of(yy, x, c)
        if i:
            arrive(r)
        pass_on(r, ax_send.at[0, i], plus)
        pass_on(r, ax_send.at[1, i], minus)
        pass_on(r, ad_send.at[i], sibling)

    def relay(i):
        yy = lax.rem(y + far[i], 8)
        rm_ = row_of(yy, xm, c)
        rp_ = row_of(yy, xp, c)
        arrive(rm_)
        if i % 2 == 0:
            pass_on(rm_, ax_send.at[2, i], plus)
        pass_on(rm_, ad_send.at[8 + i], sibling)
        arrive(rp_)
        if i % 2 == 1:
            pass_on(rp_, ax_send.at[2, i], minus)
        pass_on(rp_, ad_send.at[16 + i], sibling)

    def last(i):
        yy = lax.rem(y + far[i], 8)
        r = row_of(yy, xo, c)
        arrive(r)
        pass_on(r, ad_send.at[24 + i], sibling)

    for i in range(8):
        spread(i)
    for i in range(8):
        relay(i)
    for i in range(8):
        last(i)
    for yy in range(8):
        for xx in range(4):
            arrive(row_of(yy, xx, oc))

    for gp in range(4):
        for s in range(16):
            wide[s] = rows[gp * 16 + s].astype(F32)
        w = wide.reshape(16 * J, 128)
        for j in range(J):
            params_ref[pl.ds(gp * 16, 16), pl.ds(j * 128, 128)] = w[pl.ds(j, 16, stride=J), :].astype(BF16)

    for cp in d_copies:
        cp.wait_send()
    for cp in pending:
        cp.wait_send()
    for k in range(4):
        for cc in range(2):
            def done():
                remote(ys.at[k, cc], yr.at[0], y_send.at[k, cc], y_recv.at[0], sibling).wait_send()

            if k == 2:
                pl.when(jnp.logical_not(jnp.logical_and(c == ylo, c == cc)))(done)
            else:
                done()


def per_device(grads, master, moment, second, step):
    g = grads.reshape(8, 8, J, 128).transpose(0, 2, 1, 3)
    row = jax.ShapeDtypeStruct((J, 128), F32)
    vmem = pl.BlockSpec(memory_space=pltpu.VMEM)
    dma = pltpu.SemaphoreType.DMA
    outs = pl.pallas_call(
        kernel,
        out_shape=(row, row, row, jax.ShapeDtypeStruct((64, J * 128), BF16)),
        in_specs=[pl.BlockSpec(memory_space=pltpu.SMEM), pl.BlockSpec(memory_space=pl.ANY), vmem, vmem, vmem],
        out_specs=(vmem, vmem, vmem, vmem),
        scratch_shapes=[
            pltpu.VMEM((4, J, 8, 128), F32),
            pltpu.VMEM((4, J, 8, 128), F32),
            pltpu.VMEM((4, 4, 2, J, 128), F32),
            pltpu.VMEM((4, J, 128), F32),
            pltpu.VMEM((4, J, 128), F32),
            pltpu.VMEM((4, J, 128), F32),
            pltpu.VMEM((4, J, 128), F32),
            pltpu.VMEM((4, 2, J, 128), F32),
            pltpu.VMEM((4, 2, J, 128), F32),
            pltpu.VMEM((4, 2, J, 128), F32),
            pltpu.VMEM((8, J, 128), F32),
            pltpu.VMEM((64, J, 128), BF16),
            pltpu.VMEM((16, J, 128), F32),
            dma((4,)), dma((4,)), dma((4,)),
            dma((6, 4)), dma((6, 4)),
            dma((4, 2)), dma((8,)),
            dma((7,)), dma((64,)), dma((3, 8)), dma((32,)),
        ],
        compiler_params=pltpu.CompilerParams(collective_id=0, has_side_effects=True),
    )(step, g, master.reshape(J, 128), moment.reshape(J, 128), second.reshape(J, 128))
    new_master, new_moment, new_second, params = outs
    flat = (1, J * 128)
    return (new_master.reshape(flat), new_moment.reshape(flat), new_second.reshape(flat), params)


def solution(mesh):
    placed = (
        P(("section", "pair"), "dp", None, None),
        P(("section", "pair", "dp"), None),
        P(("section", "pair", "dp"), None),
        P(("section", "pair", "dp"), None),
        P("section"),
    )
    return jax.shard_map(
        per_device,
        mesh=mesh,
        in_specs=placed,
        out_specs=(
            P(("section", "pair", "dp"), None),
            P(("section", "pair", "dp"), None),
            P(("section", "pair", "dp"), None),
            P("section", None),
        ),
        check_vma=False,
    )
```

time: 342 us -> 59.8 us (0.17)
  the two profiles are of different devices: /device:TPU:9 before, /device:TPU:1 now
where the time goes in v1:
time: 59.8 us; the launch traced here: 59.3 us
  Pallas kernels  51.8 us (87%)
  local copies, waits for them, and re-layouts  6.23 us (10%)
  between operations  1.29 us (2%)
    pallas_call x1, Pallas kernels, per_device(): pl.pallas_call(kernel, out_shape=(row, row, row, jax.ShapeDtypeStruct((64...  51.8 us
    unnamed x4, local copies, waits for them, and re-layouts  6.23 us

profile of v1, /device:TPU:1, one launch (start us, length us, event | category | flops | bytes accessed | tf_op | source)
XLA Modules:
  0.0 59.3 jit_solution(9491492931820178045)
XLA Ops:
  1.3 51.8 %shard_map.84 = (f32[56,128]{1,0:T(8,128)}, f32[56,128]{1,0:T(8,128)}, f32[56,128]{1,0:T(8,128)}, bf16[64,7168]{1,0:T(8,128)(2,1)}) custom-call(s32[1]{0:T(128)S(6)} %copy.13.step_ref, f32[8,56,8,128]{3,2,1,0:T(8,128)} %bitcast.9, f32[56,128]{1,0:T(8,128)} %bitcast.10, f32[56,128]{1,0:T(8,128)} %bitcast.11, f32[56,128]{1,0:T(8,128)} %bitcast.12), custom_call_target="tpu_custom_call" | custom-call | tf_op jit(solution)/shard_map/pallas_call | solution.py:253
  53.1 1.4 %copy.14 = f32[1,7168]{1,0:T(1,128)} copy(f32[1,7168]{1,0:T(1,128)} %bitcast.15) | data formatting | bytes 57344
  54.4 1.4 %copy.15 = f32[1,7168]{1,0:T(1,128)} copy(f32[1,7168]{1,0:T(1,128)} %bitcast.14) | data formatting | bytes 57344
  55.8 1.4 %copy.16 = f32[1,7168]{1,0:T(1,128)} copy(f32[1,7168]{1,0:T(1,128)} %bitcast.13) | data formatting | bytes 57344
  57.2 2.2 %copy.17 = bf16[64,7168]{1,0:T(8,128)(2,1)} copy(bf16[64,7168]{1,0:T(8,128)(2,1)} %get-tuple-element.19) | data formatting | bytes 1835008

commit v2 on v0

v2 whole, which is shorter than its diff:
```python
import jax
import jax.numpy as jnp
from jax import lax
from jax.experimental import pallas as pl
from jax.experimental.pallas import tpu as pltpu
from jax.sharding import PartitionSpec as P

MESH = pl.DeviceIdType.MESH
F32 = jnp.float32
BF16 = jnp.bfloat16
I16 = jnp.int16
J = 56
CODE = 64
TOP = 32700.0
STEPS = 256.0
FAR = (1, 7, 2, 6, 3, 5, 4)


def encode(v):
    v = v.reshape(7, 8, 128)
    largest = jnp.maximum(jnp.max(jnp.abs(v), axis=0), 1e-30)
    e = jnp.ceil(jnp.log2(largest) * STEPS)
    q = jnp.round(v * (TOP * jnp.exp2(e * (-1.0 / STEPS)))[None])
    return jnp.concatenate([q.reshape(J, 128), e], axis=0).astype(jnp.int32).astype(I16)


def decode(code):
    f = code.astype(jnp.int32).astype(F32)
    scale = jnp.exp2(f[J:] * (1.0 / STEPS)) * (1.0 / TOP)
    return (f[:J].reshape(7, 8, 128) * scale[None]).reshape(J, 128)


def reduce_update_gather(
    step_hbm, g_ref, master_hbm, moment_hbm, second_hbm,
    new_master_ref, new_moment_ref, new_second_ref, rows,
    mine, sib, xs, xcode, xin, ycode, yin, state, step_ref,
    load_sem, state_sem, d_send, d_recv, x_send, x_recv, y_send, y_recv,
    ay_send, a_recv, ax_send, ad_send,
):
    ylo = lax.axis_index("pair")
    dp = lax.axis_index("dp")
    c = lax.rem(dp, 2)
    x = lax.rem(dp // 2, 4)
    yhi = dp // 8
    y = yhi * 2 + ylo
    oc = 1 - c
    xp = lax.rem(x + 1, 4)
    xm = lax.rem(x + 3, 4)
    xo = lax.rem(x + 2, 4)

    def dev(yy, xx, cc):
        return {"pair": lax.rem(yy, 2), "dp": ((yy // 2) * 4 + xx) * 2 + cc}

    sibling = dev(y, x, oc)
    across = [dev(y, xx, c) for xx in (xo, xp, xm)]

    def remote(src, dst, ssem, rsem, where):
        return pltpu.make_async_remote_copy(
            src_ref=src, dst_ref=dst, send_sem=ssem, recv_sem=rsem,
            device_id=where, device_id_type=MESH,
        )

    barrier = pltpu.get_barrier_semaphore()
    for where in [sibling] + across:
        pl.semaphore_signal(barrier, inc=1, device_id=where, device_id_type=MESH)
    for d in FAR:
        yy = lax.rem(y + d, 8)
        for cc in range(2):
            pl.semaphore_signal(barrier, inc=1, device_id=dev(yy, x, cc), device_id_type=MESH)

    hi_of = [lax.rem(yhi + d, 4) for d in (2, 1, 3, 0)]
    loads = []
    for k in range(4):
        cp = pltpu.make_async_copy(g_ref.at[c * 4 + hi_of[k]], mine.at[k], load_sem.at[k])
        cp.start()
        loads.append(cp)
    state_copies = [
        pltpu.make_async_copy(src, dst, state_sem.at[i])
        for i, (src, dst) in enumerate((
            (step_hbm, step_ref), (master_hbm, state.at[0]), (moment_hbm, state.at[1]), (second_hbm, state.at[2]),
        ))
    ]
    for cp in state_copies:
        cp.start()

    pl.semaphore_wait(barrier, 18)

    pending = []

    def send(*args):
        cp = remote(*args)
        cp.start()
        pending.append(cp)
        return cp

    d_copies = [
        send(g_ref.at[oc * 4 + hi_of[k]], sib.at[k], d_send.at[k], d_recv.at[k], sibling) for k in range(4)
    ]
    x_copies = {}

    def stage_sum(k):
        loads[k].wait()
        d_copies[k].wait_recv()
        a = mine.at[k].reshape(J * 8, 128)
        b = sib.at[k].reshape(J * 8, 128)

        def summed(xx, cc):
            pieces = []
            for jb in range(7):
                sl = pl.ds(jb * 64 + xx * 2 + cc, 8, stride=8)
                pieces.append(a[sl, :] + b[sl, :])
            return jnp.concatenate(pieces, axis=0)

        for i, xx in enumerate((xo, xp, xm)):
            for cc in range(2):
                xcode[k, i, cc] = encode(summed(xx, cc))
            x_copies[k, i] = send(xcode.at[k, i], xin.at[k, i], x_send.at[k, i], x_recv.at[k, i], across[i])
        for cc in range(2):
            xs[k, cc] = summed(x, cc)

    def stage_y(k):
        yy = hi_of[k] * 2 + c
        for i in range(3):
            x_copies[k, i].wait_recv()
        for cc in range(2):
            ycode[k, cc] = encode(
                xs[k, cc] + decode(xin[k, 1, cc]) + decode(xin[k, 2, cc]) + decode(xin[k, 0, cc])
            )

            def start():
                remote(ycode.at[k, cc], yin.at[y], y_send.at[k, cc], y_recv.at[y], dev(yy, x, cc)).start()

            if k == 3:
                own = jnp.logical_and(c == ylo, c == cc)

                @pl.when(own)
                def _():
                    yin[y] = ycode[k, cc]

                pl.when(jnp.logical_not(own))(start)
            else:
                start()

    stage_sum(0)
    stage_sum(1)
    stage_sum(2)
    stage_sum(3)
    stage_y(0)
    stage_y(1)
    stage_y(2)
    stage_y(3)

    for cp in state_copies:
        cp.wait()
    t = step_ref[0]
    p1 = jnp.float32(1.0)
    p2 = jnp.float32(1.0)
    b1, b2 = 0.9, 0.95
    for bit in range(8):
        on = lax.rem(lax.shift_right_logical(t, bit), 2) == 1
        p1 = p1 * jnp.where(on, jnp.float32(b1), jnp.float32(1.0))
        p2 = p2 * jnp.where(on, jnp.float32(b2), jnp.float32(1.0))
        b1, b2 = b1 * b1, b2 * b2
    first_fix = jnp.full((J, 128), 1.0 - p1, F32)
    second_fix = jnp.full((J, 128), 1.0 - p2, F32)

    def y_wait(slot):
        remote(ycode.at[0, 0], yin.at[slot], y_send.at[0, 0], y_recv.at[slot], sibling).wait_recv()

    @pl.when(c != ylo)
    def _():
        y_wait(y)

    for d in FAR[::-1]:
        y_wait(lax.rem(y + d, 8))
    total = decode(yin[0])
    for i in range(1, 8):
        total = total + decode(yin[i])

    master = state[0]
    new_moment = 0.9 * state[1] + 0.1 * total
    new_second = 0.95 * state[2] + 0.05 * total * total
    update = new_moment / first_fix / (jnp.sqrt(new_second / second_fix) + 1e-08) + 0.1 * master
    new_master = master - 0.03 * update

    def row_of(yy, xx, cc):
        return lax.rem(yy, 2) * 32 + (yy // 2) * 8 + xx * 2 + cc

    me = row_of(y, x, c)
    rows[me] = new_master.astype(BF16)

    def pass_on(r, sem, where):
        send(rows.at[r], rows.at[r], sem, a_recv.at[r], where)

    def arrive(r):
        remote(rows.at[r], rows.at[r], ad_send.at[0], a_recv.at[r], sibling).wait_recv()

    for i, d in enumerate(FAR):
        pass_on(me, ay_send.at[i], dev(lax.rem(y + d, 8), x, c))

    def spread(i):
        r = row_of(lax.rem(y + ((0,) + FAR)[i], 8), x, c)
        if i:
            arrive(r)
        for q in range(3):
            pass_on(r, ax_send.at[q, i], across[q])
        pass_on(r, ad_send.at[i], sibling)

    def collect(i):
        yy = lax.rem(y + ((0,) + FAR)[i], 8)
        for q, xx in enumerate((xp, xm, xo)):
            r = row_of(yy, xx, c)
            arrive(r)
            pass_on(r, ad_send.at[8 + 3 * i + q], sibling)

    for i in range(8):
        spread(i)
    new_master_ref[...] = new_master
    new_moment_ref[...] = new_moment
    new_second_ref[...] = new_second
    for i in range(8):
        collect(i)
    for yy in range(8):
        for xx in range(4):
            arrive(row_of(yy, xx, oc))

    for cp in pending:
        cp.wait_send()
    for k in range(4):
        for cc in range(2):
            def done():
                remote(ycode.at[k, cc], yin.at[0], y_send.at[k, cc], y_recv.at[0], sibling).wait_send()

            if k == 3:
                pl.when(jnp.logical_not(jnp.logical_and(c == ylo, c == cc)))(done)
            else:
                done()


def write_out(
    m_ref, v_ref, s_ref, rows, m_out, v_out, s_out, p_out, wide, tiles, sems, tile_sems,
):
    small = [
        pltpu.make_async_copy(src, dst, sems.at[i])
        for i, (src, dst) in enumerate(((m_ref, m_out), (v_ref, v_out), (s_ref, s_out)))
    ]
    for cp in small:
        cp.start()
    copies = []
    for gp in range(4):
        for s in range(16):
            wide[gp % 2, s] = rows[gp * 16 + s].astype(F32)
        w = wide.at[gp % 2].reshape(16 * J, 128)
        for j in range(J):
            tiles[gp, :, pl.ds(j * 128, 128)] = w[pl.ds(j, 16, stride=J), :].astype(BF16)
        cp = pltpu.make_async_copy(tiles.at[gp], p_out.at[pl.ds(gp * 16, 16), :], tile_sems.at[gp])
        cp.start()
        copies.append(cp)
    for cp in small + copies:
        cp.wait()


def per_device(grads, master, moment, second, step):
    g = grads.reshape(8, 8, J, 128).transpose(0, 2, 1, 3)
    row = jax.ShapeDtypeStruct((J, 128), F32)
    vmem = pl.BlockSpec(memory_space=pltpu.VMEM)
    hbm = pl.BlockSpec(memory_space=pltpu.HBM)
    dma = pltpu.SemaphoreType.DMA
    parts = pl.pallas_call(
        reduce_update_gather,
        out_shape=(row, row, row, jax.ShapeDtypeStruct((64, J, 128), BF16)),
        in_specs=[hbm] * 5,
        out_specs=(vmem,) * 4,
        scratch_shapes=[
            pltpu.VMEM((4, J, 8, 128), F32),
            pltpu.VMEM((4, J, 8, 128), F32),
            pltpu.VMEM((4, 2, J, 128), F32),
            pltpu.VMEM((4, 3, 2, CODE, 128), I16),
            pltpu.VMEM((4, 3, 2, CODE, 128), I16),
            pltpu.VMEM((4, 2, CODE, 128), I16),
            pltpu.VMEM((8, CODE, 128), I16),
            pltpu.VMEM((3, J, 128), F32),
            pltpu.SMEM((1,), jnp.int32),
            dma((4,)), dma((4,)), dma((4,)), dma((4,)),
            dma((4, 3)), dma((4, 3)),
            dma((4, 2)), dma((8,)),
            dma((7,)), dma((64,)), dma((3, 8)), dma((32,)),
        ],
        compiler_params=pltpu.CompilerParams(
            collective_id=0, has_side_effects=True, vmem_limit_bytes=54500000
        ),
    )(step, g, master.reshape(J, 128), moment.reshape(J, 128), second.reshape(J, 128))
    new_master, new_moment, new_second, params = pl.pallas_call(
        write_out,
        out_shape=(row, row, row, jax.ShapeDtypeStruct((64, J * 128), BF16)),
        in_specs=[vmem] * 4,
        out_specs=(hbm,) * 4,
        scratch_shapes=[
            pltpu.VMEM((2, 16, J, 128), F32),
            pltpu.VMEM((4, 16, J * 128), BF16),
            dma((3,)), dma((4,)),
        ],
        compiler_params=pltpu.CompilerParams(vmem_limit_bytes=24 << 20),
    )(*parts)
    flat = (1, J * 128)
    return (new_master.reshape(flat), new_moment.reshape(flat), new_second.reshape(flat), params)


def solution(mesh):
    placed = (
        P(("section", "pair"), "dp", None, None),
        P(("section", "pair", "dp"), None),
        P(("section", "pair", "dp"), None),
        P(("section", "pair", "dp"), None),
        P("section"),
    )
    return jax.shard_map(
        per_device,
        mesh=mesh,
        in_specs=placed,
        out_specs=(
            P(("section", "pair", "dp"), None),
            P(("section", "pair", "dp"), None),
            P(("section", "pair", "dp"), None),
            P("section", None),
        ),
        check_vma=False,
    )
```

time: 342 us -> 46.8 us (0.14)
  the two profiles are of different devices: /device:TPU:9 before, /device:TPU:1 now
where the time goes in v2:
time: 46.8 us; the launch traced here: 46.4 us
  Pallas kernels  42.9 us (92%)
  local copies, waits for them, and re-layouts  2.24 us (5%)
  between operations  1.3 us (3%)
    pallas_call x1, Pallas kernels, per_device(): pl.pallas_call(reduce_update_gather, out_shape=(row, row, row, jax.ShapeD...  41.7 us
    unnamed x6, local copies, waits for them, and re-layouts  2.24 us
    pallas_call x1, Pallas kernels, per_device(): pl.pallas_call(write_out, out_shape=(row, row, row, jax.ShapeDtypeStruct(...  1.21 us

profile of v2, /device:TPU:1, one launch (start us, length us, event | category | flops | bytes accessed | tf_op | source)
XLA Modules:
  0.0 46.4 jit_solution(556283487220360637)
XLA Ops:
  1.3 0.0 copy-start
  1.3 0.7 %copy-done = f32[1,7168]{1,0:T(1,128)S(1)} copy-done((f32[1,7168]{1,0:T(1,128)S(1)}, f32[1,7168]{1,0:T(1,128)}, u32[]{:S(2)}) %copy-start) | copy-done | bytes 28696
  2.0 0.0 copy-start.1
  2.0 0.7 %copy-done.1 = f32[1,7168]{1,0:T(1,128)S(1)} copy-done((f32[1,7168]{1,0:T(1,128)S(1)}, f32[1,7168]{1,0:T(1,128)}, u32[]{:S(2)}) %copy-start.1) | copy-done | bytes 28696
  2.8 0.0 copy-start.2
  2.8 0.7 %copy-done.2 = f32[1,7168]{1,0:T(1,128)S(1)} copy-done((f32[1,7168]{1,0:T(1,128)S(1)}, f32[1,7168]{1,0:T(1,128)}, u32[]{:S(2)}) %copy-start.2) | copy-done | bytes 28696
  3.5 41.7 %shard_map.84 = (f32[56,128]{1,0:T(8,128)S(1)}, f32[56,128]{1,0:T(8,128)S(1)}, f32[56,128]{1,0:T(8,128)S(1)}, bf16[64,56,128]{2,1,0:T(8,128)(2,1)S(1)}) custom-call(s32[1]{0:T(128)S(6)} %copy.9.step_hbm, f32[8,56,8,128]{3,2,1,0:T(8,128)} %bitcast.12, f32[56,128]{1,0:T(8,128)S(1)} %bitcast.9, f32[56,128]{1,0:T(8,128)S(1)} %bitcast.10, f32[56,128]{1,0:T(8,128)S(1)} %bitcast.11), custom_call_target="tpu_custom_call" | custom-call | tf_op jit(solution)/shard_map/pallas_call | solution.py:269
  45.2 1.2 %shard_map.85 = (f32[56,128]{1,0:T(8,128)}, f32[56,128]{1,0:T(8,128)}, f32[56,128]{1,0:T(8,128)}, bf16[64,7168]{1,0:T(8,128)(2,1)}) custom-call(f32[56,128]{1,0:T(8,128)S(1)} %get-tuple-element.12.m_ref, f32[56,128]{1,0:T(8,128)S(1)} %get-tuple-element.13.v_ref, f32[56,128]{1,0:T(8,128)S(1)} %get-tuple-element.14.s_ref, ...), custom_call_target="tpu_custom_call" | custom-call | tf_op jit(solution)/shard_map/pallas_call | solution.py:293
Async XLA Ops:
  1.3 0.7 %copy-start = (f32[1,7168]{1,0:T(1,128)S(1)}, f32[1,7168]{1,0:T(1,128)}, u32[]{:S(2)}) copy-start(f32[1,7168]{1,0:T(1,128)} %param.6) | copy-start | bytes 86020
  2.0 0.7 %copy-start.1 = (f32[1,7168]{1,0:T(1,128)S(1)}, f32[1,7168]{1,0:T(1,128)}, u32[]{:S(2)}) copy-start(f32[1,7168]{1,0:T(1,128)} %param.7) | copy-start | bytes 86020
  2.8 0.7 %copy-start.2 = (f32[1,7168]{1,0:T(1,128)S(1)}, f32[1,7168]{1,0:T(1,128)}, u32[]{:S(2)}) copy-start(f32[1,7168]{1,0:T(1,128)} %param.8) | copy-start | bytes 86020

commit v3 on v2

--- a/solution.py
+++ b/solution.py
@@ -14,6 +14,8 @@
 TOP = 32700.0
 STEPS = 256.0
 FAR = (1, 7, 2, 6, 3, 5, 4)
+Y_ORDER = (4, 3, 5, 1, 7, 2, 6)
+A_ORDER = ("c1", "c7", "o", "c2", "c6", "c3", "c5", "c4", "b", "g1", "g7", "g2", "g6", "k", "g3", "g5", "g4")
 
 
 def encode(v):
@@ -31,11 +33,10 @@
 
 
 def reduce_update_gather(
-    step_hbm, g_ref, master_hbm, moment_hbm, second_hbm,
+    step_ref, g_ref, master_hbm, moment_hbm, second_hbm,
     new_master_ref, new_moment_ref, new_second_ref, rows,
-    mine, sib, xs, xcode, xin, ycode, yin, state, step_ref,
-    load_sem, state_sem, d_send, d_recv, x_send, x_recv, y_send, y_recv,
-    ay_send, a_recv, ax_send, ad_send,
+    mine, sib, xs, xcode, xin, ycode, yin, state,
+    load_sem, state_sem, sent, d_recv, x_recv, y_recv, a_recv,
 ):
     ylo = lax.axis_index("pair")
     dp = lax.axis_index("dp")
@@ -60,6 +61,9 @@
             device_id=where, device_id_type=MESH,
         )
 
+    def wait_for(ref, sem):
+        pltpu.make_async_copy(ref, ref, sem).wait()
+
     barrier = pltpu.get_barrier_semaphore()
     for where in [sibling] + across:
         pl.semaphore_signal(barrier, inc=1, device_id=where, device_id_type=MESH)
@@ -69,38 +73,19 @@
             pl.semaphore_signal(barrier, inc=1, device_id=dev(yy, x, cc), device_id_type=MESH)
 
     hi_of = [lax.rem(yhi + d, 4) for d in (2, 1, 3, 0)]
-    loads = []
     for k in range(4):
-        cp = pltpu.make_async_copy(g_ref.at[c * 4 + hi_of[k]], mine.at[k], load_sem.at[k])
-        cp.start()
-        loads.append(cp)
-    state_copies = [
-        pltpu.make_async_copy(src, dst, state_sem.at[i])
-        for i, (src, dst) in enumerate((
-            (step_hbm, step_ref), (master_hbm, state.at[0]), (moment_hbm, state.at[1]), (second_hbm, state.at[2]),
-        ))
-    ]
-    for cp in state_copies:
-        cp.start()
+        pltpu.make_async_copy(g_ref.at[c * 4 + hi_of[k]], mine.at[k], load_sem.at[k]).start()
+    for i, src in enumerate((master_hbm, moment_hbm, second_hbm)):
+        pltpu.make_async_copy(src, state.at[i], state_sem).start()
 
     pl.semaphore_wait(barrier, 18)
 
-    pending = []
-
-    def send(*args):
-        cp = remote(*args)
-        cp.start()
-        pending.append(cp)
-        return cp
-
-    d_copies = [
-        send(g_ref.at[oc * 4 + hi_of[k]], sib.at[k], d_send.at[k], d_recv.at[k], sibling) for k in range(4)
-    ]
-    x_copies = {}
+    for k in range(4):
+        remote(g_ref.at[oc * 4 + hi_of[k]], sib.at[k], sent.at[0], d_recv.at[k], sibling).start()
 
     def stage_sum(k):
-        loads[k].wait()
-        d_copies[k].wait_recv()
+        wait_for(mine.at[k], load_sem.at[k])
+        wait_for(sib.at[k], d_recv.at[k])
         a = mine.at[k].reshape(J * 8, 128)
         b = sib.at[k].reshape(J * 8, 128)
 
@@ -114,21 +99,20 @@
         for i, xx in enumerate((xo, xp, xm)):
             for cc in range(2):
                 xcode[k, i, cc] = encode(summed(xx, cc))
-            x_copies[k, i] = send(xcode.at[k, i], xin.at[k, i], x_send.at[k, i], x_recv.at[k, i], across[i])
+            remote(xcode.at[k, i], xin.at[k, i], sent.at[1], x_recv.at[k], across[i]).start()
         for cc in range(2):
             xs[k, cc] = summed(x, cc)
 
     def stage_y(k):
         yy = hi_of[k] * 2 + c
-        for i in range(3):
-            x_copies[k, i].wait_recv()
+        wait_for(xin.at[k], x_recv.at[k])
         for cc in range(2):
             ycode[k, cc] = encode(
                 xs[k, cc] + decode(xin[k, 1, cc]) + decode(xin[k, 2, cc]) + decode(xin[k, 0, cc])
             )
 
             def start():
-                remote(ycode.at[k, cc], yin.at[y], y_send.at[k, cc], y_recv.at[y], dev(yy, x, cc)).start()
+                remote(ycode.at[k, cc], yin.at[y], sent.at[2], y_recv, dev(yy, x, cc)).start()
 
             if k == 3:
                 own = jnp.logical_and(c == ylo, c == cc)
@@ -145,13 +129,8 @@
     stage_sum(1)
     stage_sum(2)
     stage_sum(3)
-    stage_y(0)
-    stage_y(1)
-    stage_y(2)
-    stage_y(3)
-
-    for cp in state_copies:
-        cp.wait()
+
+    wait_for(state, state_sem)
     t = step_ref[0]
     p1 = jnp.float32(1.0)
     p2 = jnp.float32(1.0)
@@ -164,15 +143,21 @@
     first_fix = jnp.full((J, 128), 1.0 - p1, F32)
     second_fix = jnp.full((J, 128), 1.0 - p2, F32)
 
-    def y_wait(slot):
-        remote(ycode.at[0, 0], yin.at[slot], y_send.at[0, 0], y_recv.at[slot], sibling).wait_recv()
-
-    @pl.when(c != ylo)
-    def _():
-        y_wait(y)
-
-    for d in FAR[::-1]:
-        y_wait(lax.rem(y + d, 8))
+    stage_y(0)
+    stage_y(1)
+    stage_y(2)
+    stage_y(3)
+
+    def seven_or_eight(sem):
+        @pl.when(c == ylo)
+        def _():
+            wait_for(yin.at[pl.ds(0, 7)], sem)
+
+        @pl.when(c != ylo)
+        def _():
+            wait_for(yin, sem)
+
+    seven_or_eight(y_recv)
     total = decode(yin[0])
     for i in range(1, 8):
         total = total + decode(yin[i])
@@ -186,55 +171,78 @@
     def row_of(yy, xx, cc):
         return lax.rem(yy, 2) * 32 + (yy // 2) * 8 + xx * 2 + cc
 
+    slot = {d: i for i, d in enumerate((1, 2, 3, 4, 5, 6, 7))}
+    COLUMN, GROUP, OPPOSITE, BESIDE, CORNER, SIBLING = 0, 7, 14, 15, 16, 17
+    NEAR = (1, 7, 2, 6)
+
+    def at_y(d):
+        return lax.rem(y + d, 8)
+
+    def pass_on(r, index, where):
+        remote(rows.at[r], rows.at[r], sent.at[3], a_recv.at[index], where).start()
+
+    def arrived(n, index):
+        wait_for(rows.at[pl.ds(0, n)], a_recv.at[index])
+
     me = row_of(y, x, c)
     rows[me] = new_master.astype(BF16)
-
-    def pass_on(r, sem, where):
-        send(rows.at[r], rows.at[r], sem, a_recv.at[r], where)
-
-    def arrive(r):
-        remote(rows.at[r], rows.at[r], ad_send.at[0], a_recv.at[r], sibling).wait_recv()
-
-    for i, d in enumerate(FAR):
-        pass_on(me, ay_send.at[i], dev(lax.rem(y + d, 8), x, c))
-
-    def spread(i):
-        r = row_of(lax.rem(y + ((0,) + FAR)[i], 8), x, c)
-        if i:
-            arrive(r)
-        for q in range(3):
-            pass_on(r, ax_send.at[q, i], across[q])
-        pass_on(r, ad_send.at[i], sibling)
-
-    def collect(i):
-        yy = lax.rem(y + ((0,) + FAR)[i], 8)
-        for q, xx in enumerate((xp, xm, xo)):
-            r = row_of(yy, xx, c)
-            arrive(r)
-            pass_on(r, ad_send.at[8 + 3 * i + q], sibling)
-
-    for i in range(8):
-        spread(i)
+    for d in Y_ORDER:
+        pass_on(me, COLUMN + slot[8 - d], dev(at_y(d), x, c))
+    pass_on(me, OPPOSITE, across[0])
+    pass_on(me, BESIDE, across[1])
+    pass_on(me, BESIDE, across[2])
+    pass_on(me, SIBLING, sibling)
+
+    def column(d):
+        arrived(1, COLUMN + slot[d])
+        r = row_of(at_y(d), x, c)
+        if d not in NEAR:
+            pass_on(r, GROUP + slot[d], across[0])
+        pass_on(r, GROUP + slot[d], across[1])
+        pass_on(r, GROUP + slot[d], across[2])
+        pass_on(r, SIBLING, sibling)
+
+    def opposite():
+        arrived(1, OPPOSITE)
+        r = row_of(y, xo, c)
+        for d in NEAR:
+            pass_on(r, CORNER, dev(at_y(d), x, c))
+        pass_on(r, SIBLING, sibling)
+
+    def group(d):
+        arrived(2 if d in NEAR else 3, GROUP + slot[d])
+        pass_on(row_of(at_y(d), xp, c), SIBLING, sibling)
+        pass_on(row_of(at_y(d), xm, c), SIBLING, sibling)
+        if d not in NEAR:
+            pass_on(row_of(at_y(d), xo, c), SIBLING, sibling)
+
+    def beside():
+        arrived(2, BESIDE)
+        pass_on(row_of(y, xp, c), SIBLING, sibling)
+        pass_on(row_of(y, xm, c), SIBLING, sibling)
+
+    def corner():
+        arrived(4, CORNER)
+        for d in NEAR:
+            pass_on(row_of(at_y(d), xo, c), SIBLING, sibling)
+
+    steps = {"o": opposite, "b": beside, "k": corner}
+    for what in A_ORDER:
+        if what in steps:
+            steps[what]()
+        elif what[0] == "c":
+            column(int(what[1]))
+        else:
+            group(int(what[1]))
     new_master_ref[...] = new_master
     new_moment_ref[...] = new_moment
     new_second_ref[...] = new_second
-    for i in range(8):
-        collect(i)
-    for yy in range(8):
-        for xx in range(4):
-            arrive(row_of(yy, xx, oc))
-
-    for cp in pending:
-        cp.wait_send()
-    for k in range(4):
-        for cc in range(2):
-            def done():
-                remote(ycode.at[k, cc], yin.at[0], y_send.at[k, cc], y_recv.at[0], sibling).wait_send()
-
-            if k == 3:
-                pl.when(jnp.logical_not(jnp.logical_and(c == ylo, c == cc)))(done)
-            else:
-                done()
+    arrived(32, SIBLING)
+
+    wait_for(sib, sent.at[0])
+    wait_for(xcode, sent.at[1])
+    seven_or_eight(sent.at[2])
+    wait_for(rows.at[pl.ds(0, 63)], sent.at[3])
 
 
 def write_out(
@@ -269,7 +277,7 @@
     parts = pl.pallas_call(
         reduce_update_gather,
         out_shape=(row, row, row, jax.ShapeDtypeStruct((64, J, 128), BF16)),
-        in_specs=[hbm] * 5,
+        in_specs=[pl.BlockSpec(memory_space=pltpu.SMEM)] + [hbm] * 4,
         out_specs=(vmem,) * 4,
         scratch_shapes=[
             pltpu.VMEM((4, J, 8, 128), F32),
@@ -280,16 +288,15 @@
             pltpu.VMEM((4, 2, CODE, 128), I16),
             pltpu.VMEM((8, CODE, 128), I16),
             pltpu.VMEM((3, J, 128), F32),
-            pltpu.SMEM((1,), jnp.int32),
-            dma((4,)), dma((4,)), dma((4,)), dma((4,)),
-            dma((4, 3)), dma((4, 3)),
-            dma((4, 2)), dma((8,)),
-            dma((7,)), dma((64,)), dma((3, 8)), dma((32,)),
+            dma((4,)), dma, dma((4,)), dma((4,)), dma((4,)), dma, dma((18,)),
         ],
         compiler_params=pltpu.CompilerParams(
-            collective_id=0, has_side_effects=True, vmem_limit_bytes=54500000
+            collective_id=0, has_side_effects=True, vmem_limit_bytes=24 << 20
         ),
-    )(step, g, master.reshape(J, 128), moment.reshape(J, 128), second.reshape(J, 128))
+    )(step, *[
+        pltpu.with_memory_space_constraint(a, pltpu.HBM)
+        for a in (g, master.reshape(J, 128), moment.reshape(J, 128), second.reshape(J, 128))
+    ])
     new_master, new_moment, new_second, params = pl.pallas_call(
         write_out,
         out_shape=(row, row, row, jax.ShapeDtypeStruct((64, J * 128), BF16)),

time: 46.8 us -> 42.8 us (0.915)
  local copies, waits for them, and re-layouts: 2.24 us -> 0 us
  Pallas kernels: 42.9 us -> 41.3 us
    unnamed x6 -> x0, local copies, waits for them, and re-layouts: 2.24 us -> none
    pallas_call x1, Pallas kernels: 41.7 us -> 40.1 us  [per_device(): pl.pallas_call(reduce_update_gather, out_shape=(row, row, row, jax.ShapeD...]
where the time goes in v3:
time: 42.8 us; the launch traced here: 42.6 us
  Pallas kernels  41.3 us (96%)
  between operations  1.29 us (3%)
    pallas_call x1, Pallas kernels, per_device(): pl.pallas_call(reduce_update_gather, out_shape=(row, row, row, jax.ShapeD...  40.1 us
    pallas_call x1, Pallas kernels, per_device(): pl.pallas_call(write_out, out_shape=(row, row, row, jax.ShapeDtypeStruct(...  1.22 us

profile of v3, /device:TPU:1, one launch (start us, length us, event | category | flops | bytes accessed | tf_op | source)
XLA Modules:
  0.0 42.6 jit_solution(10753481752433110885)
XLA Ops:
  1.3 40.1 %shard_map.84 = (f32[56,128]{1,0:T(8,128)S(1)}, f32[56,128]{1,0:T(8,128)S(1)}, f32[56,128]{1,0:T(8,128)S(1)}, bf16[64,56,128]{2,1,0:T(8,128)(2,1)S(1)}) custom-call(s32[1]{0:T(128)S(6)} %copy.9.step_ref, f32[8,56,8,128]{3,2,1,0:T(8,128)} %bitcast.9, f32[56,128]{1,0:T(8,128)} %bitcast.10, f32[56,128]{1,0:T(8,128)} %bitcast.11, f32[56,128]{1,0:T(8,128)} %bitcast.12), custom_call_target="tpu_custom_call" | custom-call | tf_op jit(solution)/shard_map/pallas_call | solution.py:277
  41.4 1.2 %shard_map.85 = (f32[56,128]{1,0:T(8,128)}, f32[56,128]{1,0:T(8,128)}, f32[56,128]{1,0:T(8,128)}, bf16[64,7168]{1,0:T(8,128)(2,1)}) custom-call(f32[56,128]{1,0:T(8,128)S(1)} %get-tuple-element.12.m_ref, f32[56,128]{1,0:T(8,128)S(1)} %get-tuple-element.13.v_ref, f32[56,128]{1,0:T(8,128)S(1)} %get-tuple-element.14.s_ref, ...), custom_call_target="tpu_custom_call" | custom-call | tf_op jit(solution)/shard_map/pallas_call | solution.py:300

commit v4 on v3

--- a/solution.py
+++ b/solution.py
@@ -36,7 +36,7 @@
     step_ref, g_ref, master_hbm, moment_hbm, second_hbm,
     new_master_ref, new_moment_ref, new_second_ref, rows,
     mine, sib, xs, xcode, xin, ycode, yin, state,
-    load_sem, state_sem, sent, d_recv, x_recv, y_recv, a_recv,
+    load_sem, state_sem, sent, d_recv, x_recv, y_recv, a_recv, ready, told,
 ):
     ylo = lax.axis_index("pair")
     dp = lax.axis_index("dp")
@@ -64,13 +64,19 @@
     def wait_for(ref, sem):
         pltpu.make_async_copy(ref, ref, sem).wait()
 
+    column_of = [dev(lax.rem(y + d, 8), x, 1) for d in FAR]
+    row_mates = [dev(y, xx, 1) for xx in (xo, xp, xm)]
+
+    def signal(sem, where):
+        pl.semaphore_signal(sem, inc=1, device_id=where, device_id_type=MESH)
+
     barrier = pltpu.get_barrier_semaphore()
-    for where in [sibling] + across:
-        pl.semaphore_signal(barrier, inc=1, device_id=where, device_id_type=MESH)
-    for d in FAR:
-        yy = lax.rem(y + d, 8)
-        for cc in range(2):
-            pl.semaphore_signal(barrier, inc=1, device_id=dev(yy, x, cc), device_id_type=MESH)
+    signal(barrier, sibling)
+
+    @pl.when(c == 1)
+    def _():
+        for where in row_mates + column_of:
+            signal(barrier, where)
 
     hi_of = [lax.rem(yhi + d, 4) for d in (2, 1, 3, 0)]
     for k in range(4):
@@ -78,10 +84,36 @@
     for i, src in enumerate((master_hbm, moment_hbm, second_hbm)):
         pltpu.make_async_copy(src, state.at[i], state_sem).start()
 
-    pl.semaphore_wait(barrier, 18)
+    @pl.when(c == 1)
+    def _():
+        pl.semaphore_wait(barrier, 11)
+
+    @pl.when(c == 0)
+    def _():
+        pl.semaphore_wait(barrier, 1)
 
     for k in range(4):
         remote(g_ref.at[oc * 4 + hi_of[k]], sib.at[k], sent.at[0], d_recv.at[k], sibling).start()
+
+    @pl.when(c == 1)
+    def _():
+        for where in row_mates:
+            signal(ready.at[0], where)
+        for where in column_of:
+            signal(ready.at[1], where)
+
+    def tell(axis):
+        @pl.when(c == 1)
+        def _():
+            pl.semaphore_wait(ready.at[axis], (3, 7)[axis])
+            signal(told.at[axis], sibling)
+
+    def told_of(axis):
+        @pl.when(c == 0)
+        def _():
+            pl.semaphore_wait(told.at[axis], 1)
+
+    tell(0)
 
     def stage_sum(k):
         wait_for(mine.at[k], load_sem.at[k])
@@ -99,6 +131,8 @@
         for i, xx in enumerate((xo, xp, xm)):
             for cc in range(2):
                 xcode[k, i, cc] = encode(summed(xx, cc))
+            if k == 0 and i == 0:
+                told_of(0)
             remote(xcode.at[k, i], xin.at[k, i], sent.at[1], x_recv.at[k], across[i]).start()
         for cc in range(2):
             xs[k, cc] = summed(x, cc)
@@ -129,6 +163,8 @@
     stage_sum(1)
     stage_sum(2)
     stage_sum(3)
+
+    tell(1)
 
     wait_for(state, state_sem)
     t = step_ref[0]
@@ -143,6 +179,7 @@
     first_fix = jnp.full((J, 128), 1.0 - p1, F32)
     second_fix = jnp.full((J, 128), 1.0 - p2, F32)
 
+    told_of(1)
     stage_y(0)
     stage_y(1)
     stage_y(2)
@@ -289,6 +326,7 @@
             pltpu.VMEM((8, CODE, 128), I16),
             pltpu.VMEM((3, J, 128), F32),
             dma((4,)), dma, dma((4,)), dma((4,)), dma((4,)), dma, dma((18,)),
+            pltpu.SemaphoreType.REGULAR((2,)), pltpu.SemaphoreType.REGULAR((2,)),
         ],
         compiler_params=pltpu.CompilerParams(
             collective_id=0, has_side_effects=True, vmem_limit_bytes=24 << 20

time: 42.8 us -> 40.3 us (0.942)
  Pallas kernels: 41.3 us -> 38.9 us
    pallas_call x1, Pallas kernels: 40.1 us -> 37.7 us  [per_device(): pl.pallas_call(reduce_update_gather, out_shape=(row, row, row, jax.ShapeD...]
where the time goes in v4:
time: 40.3 us; the launch traced here: 40.2 us
  Pallas kernels  38.9 us (97%)
  between operations  1.29 us (3%)
    pallas_call x1, Pallas kernels, per_device(): pl.pallas_call(reduce_update_gather, out_shape=(row, row, row, jax.ShapeD...  37.7 us
    pallas_call x1, Pallas kernels, per_device(): pl.pallas_call(write_out, out_shape=(row, row, row, jax.ShapeDtypeStruct(...  1.22 us

profile of v4, /device:TPU:1, one launch (start us, length us, event | category | flops | bytes accessed | tf_op | source)
XLA Modules:
  0.0 40.2 jit_solution(15482613984821603049)
XLA Ops:
  1.3 37.7 %shard_map.84 = (f32[56,128]{1,0:T(8,128)S(1)}, f32[56,128]{1,0:T(8,128)S(1)}, f32[56,128]{1,0:T(8,128)S(1)}, bf16[64,56,128]{2,1,0:T(8,128)(2,1)S(1)}) custom-call(s32[1]{0:T(128)S(6)} %copy.9.step_ref, f32[8,56,8,128]{3,2,1,0:T(8,128)} %bitcast.9, f32[56,128]{1,0:T(8,128)} %bitcast.10, f32[56,128]{1,0:T(8,128)} %bitcast.11, f32[56,128]{1,0:T(8,128)} %bitcast.12), custom_call_target="tpu_custom_call" | custom-call | tf_op jit(solution)/shard_map/pallas_call | solution.py:314
  39.0 1.2 %shard_map.85 = (f32[56,128]{1,0:T(8,128)}, f32[56,128]{1,0:T(8,128)}, f32[56,128]{1,0:T(8,128)}, bf16[64,7168]{1,0:T(8,128)(2,1)}) custom-call(f32[56,128]{1,0:T(8,128)S(1)} %get-tuple-element.12.m_ref, f32[56,128]{1,0:T(8,128)S(1)} %get-tuple-element.13.v_ref, f32[56,128]{1,0:T(8,128)S(1)} %get-tuple-element.14.s_ref, ...), custom_call_target="tpu_custom_call" | custom-call | tf_op jit(solution)/shard_map/pallas_call | solution.py:338

commit v5 on v4

--- a/solution.py
+++ b/solution.py
@@ -78,7 +78,7 @@
         for where in row_mates + column_of:
             signal(barrier, where)
 
-    hi_of = [lax.rem(yhi + d, 4) for d in (2, 1, 3, 0)]
+    hi_of = [lax.rem(yhi + d, 4) for d in (2, 3, 1, 0)]
     for k in range(4):
         pltpu.make_async_copy(g_ref.at[c * 4 + hi_of[k]], mine.at[k], load_sem.at[k]).start()
     for i, src in enumerate((master_hbm, moment_hbm, second_hbm)):
@@ -97,23 +97,22 @@
 
     @pl.when(c == 1)
     def _():
-        for where in row_mates:
-            signal(ready.at[0], where)
+        for where, index in zip(row_mates, (0, 2, 1)):
+            signal(ready.at[index], where)
         for where in column_of:
-            signal(ready.at[1], where)
-
-    def tell(axis):
-        @pl.when(c == 1)
-        def _():
-            pl.semaphore_wait(ready.at[axis], (3, 7)[axis])
-            signal(told.at[axis], sibling)
-
-    def told_of(axis):
-        @pl.when(c == 0)
-        def _():
-            pl.semaphore_wait(told.at[axis], 1)
-
-    tell(0)
+            signal(ready.at[3], where)
+
+    def tell(index, count):
+        pl.semaphore_wait(ready.at[index], count)
+        signal(told.at[index], sibling)
+
+    for i, xx in enumerate((xo, xp, xm)):
+        @pl.when(jnp.logical_and(c == 1, xx != 0))
+        def _(i=i):
+            tell(i, 1)
+
+    def send_x(k, i):
+        remote(xcode.at[k, i], xin.at[k, i], sent.at[1], x_recv.at[k], across[i]).start()
 
     def stage_sum(k):
         wait_for(mine.at[k], load_sem.at[k])
@@ -131,9 +130,14 @@
         for i, xx in enumerate((xo, xp, xm)):
             for cc in range(2):
                 xcode[k, i, cc] = encode(summed(xx, cc))
-            if k == 0 and i == 0:
-                told_of(0)
-            remote(xcode.at[k, i], xin.at[k, i], sent.at[1], x_recv.at[k], across[i]).start()
+
+            @pl.when(xx != 0)
+            def _(i=i):
+                if k == 0:
+                    @pl.when(c == 0)
+                    def _():
+                        pl.semaphore_wait(told.at[i], 1)
+                send_x(k, i)
         for cc in range(2):
             xs[k, cc] = summed(x, cc)
 
@@ -164,7 +168,23 @@
     stage_sum(2)
     stage_sum(3)
 
-    tell(1)
+    for i, xx in enumerate((xo, xp, xm)):
+        @pl.when(xx == 0)
+        def _(i=i):
+            @pl.when(c == 1)
+            def _():
+                tell(i, 1)
+
+            @pl.when(c == 0)
+            def _():
+                pl.semaphore_wait(told.at[i], 1)
+
+            for k in range(4):
+                send_x(k, i)
+
+    @pl.when(c == 1)
+    def _():
+        tell(3, 7)
 
     wait_for(state, state_sem)
     t = step_ref[0]
@@ -179,7 +199,10 @@
     first_fix = jnp.full((J, 128), 1.0 - p1, F32)
     second_fix = jnp.full((J, 128), 1.0 - p2, F32)
 
-    told_of(1)
+    @pl.when(c == 0)
+    def _():
+        pl.semaphore_wait(told.at[3], 1)
+
     stage_y(0)
     stage_y(1)
     stage_y(2)
@@ -326,7 +349,7 @@
             pltpu.VMEM((8, CODE, 128), I16),
             pltpu.VMEM((3, J, 128), F32),
             dma((4,)), dma, dma((4,)), dma((4,)), dma((4,)), dma, dma((18,)),
-            pltpu.SemaphoreType.REGULAR((2,)), pltpu.SemaphoreType.REGULAR((2,)),
+            pltpu.SemaphoreType.REGULAR((4,)), pltpu.SemaphoreType.REGULAR((4,)),
         ],
         compiler_params=pltpu.CompilerParams(
             collective_id=0, has_side_effects=True, vmem_limit_bytes=24 << 20

time: 40.3 us -> 39.4 us (0.978)
  Pallas kernels: 38.9 us -> 38 us
    pallas_call x1, Pallas kernels: 37.7 us -> 36.8 us  [per_device(): pl.pallas_call(reduce_update_gather, out_shape=(row, row, row, jax.ShapeD...]
where the time goes in v5:
time: 39.4 us; the launch traced here: 39.3 us
  Pallas kernels  38 us (96%)
  between operations  1.29 us (3%)
    pallas_call x1, Pallas kernels, per_device(): pl.pallas_call(reduce_update_gather, out_shape=(row, row, row, jax.ShapeD...  36.8 us
    pallas_call x1, Pallas kernels, per_device(): pl.pallas_call(write_out, out_shape=(row, row, row, jax.ShapeDtypeStruct(...  1.22 us

profile of v5, /device:TPU:1, one launch (start us, length us, event | category | flops | bytes accessed | tf_op | source)
XLA Modules:
  0.0 39.3 jit_solution(2620166034181540542)
XLA Ops:
  1.3 36.8 %shard_map.84 = (f32[56,128]{1,0:T(8,128)S(1)}, f32[56,128]{1,0:T(8,128)S(1)}, f32[56,128]{1,0:T(8,128)S(1)}, bf16[64,56,128]{2,1,0:T(8,128)(2,1)S(1)}) custom-call(s32[1]{0:T(128)S(6)} %copy.9.step_ref, f32[8,56,8,128]{3,2,1,0:T(8,128)} %bitcast.9, f32[56,128]{1,0:T(8,128)} %bitcast.10, f32[56,128]{1,0:T(8,128)} %bitcast.11, f32[56,128]{1,0:T(8,128)} %bitcast.12), custom_call_target="tpu_custom_call" | custom-call | tf_op jit(solution)/shard_map/pallas_call | solution.py:337
  38.1 1.2 %shard_map.85 = (f32[56,128]{1,0:T(8,128)}, f32[56,128]{1,0:T(8,128)}, f32[56,128]{1,0:T(8,128)}, bf16[64,7168]{1,0:T(8,128)(2,1)}) custom-call(f32[56,128]{1,0:T(8,128)S(1)} %get-tuple-element.12.m_ref, f32[56,128]{1,0:T(8,128)S(1)} %get-tuple-element.13.v_ref, f32[56,128]{1,0:T(8,128)S(1)} %get-tuple-element.14.s_ref, ...), custom_call_target="tpu_custom_call" | custom-call | tf_op jit(solution)/shard_map/pallas_call | solution.py:361

commit v6 on v4

--- a/solution.py
+++ b/solution.py
@@ -35,8 +35,8 @@
 def reduce_update_gather(
     step_ref, g_ref, master_hbm, moment_hbm, second_hbm,
     new_master_ref, new_moment_ref, new_second_ref, rows,
-    mine, sib, xs, xcode, xin, ycode, yin, state,
-    load_sem, state_sem, sent, d_recv, x_recv, y_recv, a_recv, ready, told,
+    mine, sib, xs, xcode, xin, ycode, yin, din, part, state,
+    load_sem, state_sem, sent, d_recv, x_recv, y_recv, din_recv, a_recv, ready, told,
 ):
     ylo = lax.axis_index("pair")
     dp = lax.axis_index("dp")
@@ -64,6 +64,13 @@
     def wait_for(ref, sem):
         pltpu.make_async_copy(ref, ref, sem).wait()
 
+    both, either = jnp.logical_and, jnp.logical_or
+    base = y == 0
+    first = both(base, x == 0)
+    mate = both(base, x != 0)
+    above = both(x == 0, y != 0)
+    direct = [both(base, either(x == 0, xx == 0)) for xx in (xo, xp, xm)]
+
     column_of = [dev(lax.rem(y + d, 8), x, 1) for d in FAR]
     row_mates = [dev(y, xx, 1) for xx in (xo, xp, xm)]
 
@@ -78,7 +85,7 @@
         for where in row_mates + column_of:
             signal(barrier, where)
 
-    hi_of = [lax.rem(yhi + d, 4) for d in (2, 1, 3, 0)]
+    hi_of = [lax.rem(yhi + d, 4) for d in (2, 3, 1, 0)]
     for k in range(4):
         pltpu.make_async_copy(g_ref.at[c * 4 + hi_of[k]], mine.at[k], load_sem.at[k]).start()
     for i, src in enumerate((master_hbm, moment_hbm, second_hbm)):
@@ -98,22 +105,36 @@
     @pl.when(c == 1)
     def _():
         for where in row_mates:
-            signal(ready.at[0], where)
+            signal(ready.at[first.astype(jnp.int32)], where)
         for where in column_of:
-            signal(ready.at[1], where)
-
-    def tell(axis):
-        @pl.when(c == 1)
-        def _():
-            pl.semaphore_wait(ready.at[axis], (3, 7)[axis])
-            signal(told.at[axis], sibling)
-
-    def told_of(axis):
-        @pl.when(c == 0)
-        def _():
-            pl.semaphore_wait(told.at[axis], 1)
-
-    tell(0)
+            signal(ready.at[2 - first.astype(jnp.int32)], where)
+
+        @pl.when(mate)
+        def _():
+            pl.semaphore_wait(ready.at[0], 2)
+
+        @pl.when(jnp.logical_not(mate))
+        def _():
+            pl.semaphore_wait(ready.at[0], 3)
+
+        @pl.when(base)
+        def _():
+            pl.semaphore_wait(ready.at[3], 7)
+
+        @pl.when(jnp.logical_not(base))
+        def _():
+            signal(ready.at[3], dev(0, x, 1))
+
+        signal(told.at[0], sibling)
+
+    def send_direct(k, i, xx):
+        for cc in range(2):
+            remote(
+                xcode.at[k, i, cc], din.at[x], sent.at[1], din_recv, dev(hi_of[k] * 2 + c, xx, cc)
+            ).start()
+
+    def send_x(k, i):
+        remote(xcode.at[k, i], xin.at[k, i], sent.at[1], x_recv.at[k], across[i]).start()
 
     def stage_sum(k):
         wait_for(mine.at[k], load_sem.at[k])
@@ -131,40 +152,84 @@
         for i, xx in enumerate((xo, xp, xm)):
             for cc in range(2):
                 xcode[k, i, cc] = encode(summed(xx, cc))
+
             if k == 0 and i == 0:
-                told_of(0)
-            remote(xcode.at[k, i], xin.at[k, i], sent.at[1], x_recv.at[k], across[i]).start()
+                @pl.when(c == 0)
+                def _():
+                    pl.semaphore_wait(told.at[0], 1)
+
+            now = direct[i]
+            if k == 3:
+                now = both(now, jnp.logical_not(both(xx == 0, hi_of[k] * 2 + c == 0)))
+
+            @pl.when(now)
+            def _(i=i, xx=xx):
+                send_direct(k, i, xx)
+
+            @pl.when(jnp.logical_not(direct[i]))
+            def _(i=i):
+                send_x(k, i)
+
         for cc in range(2):
             xs[k, cc] = summed(x, cc)
 
     def stage_y(k):
         yy = hi_of[k] * 2 + c
-        wait_for(xin.at[k], x_recv.at[k])
+        @pl.when(jnp.logical_not(base))
+        def _():
+            wait_for(xin.at[k], x_recv.at[k])
+
+        @pl.when(mate)
+        def _():
+            wait_for(xin.at[k, pl.ds(0, 2)], x_recv.at[k])
+
+        for i, sender in enumerate((0, 2, 1)):
+            @pl.when(jnp.logical_not(direct[sender]))
+            def _(i=i):
+                for cc in range(2):
+                    xs[k, cc] = xs[k, cc] + decode(xin[k, i, cc])
+
         for cc in range(2):
-            ycode[k, cc] = encode(
-                xs[k, cc] + decode(xin[k, 1, cc]) + decode(xin[k, 2, cc]) + decode(xin[k, 0, cc])
-            )
-
-            def start():
-                remote(ycode.at[k, cc], yin.at[y], sent.at[2], y_recv, dev(yy, x, cc)).start()
-
-            if k == 3:
-                own = jnp.logical_and(c == ylo, c == cc)
+            ycode[k, cc] = encode(xs[k, cc])
+
+        if k == 3:
+            for cc in range(2):
+                own = both(c == ylo, c == cc)
 
                 @pl.when(own)
-                def _():
+                def _(cc=cc):
                     yin[y] = ycode[k, cc]
 
-                pl.when(jnp.logical_not(own))(start)
-            else:
-                start()
+                @pl.when(jnp.logical_not(either(own, both(above, yy == 0))))
+                def _(cc=cc):
+                    send_y(k, cc)
+        else:
+            @pl.when(jnp.logical_not(both(above, yy == 0)))
+            def _():
+                for cc in range(2):
+                    send_y(k, cc)
+
+    def send_y(k, cc):
+        remote(
+            ycode.at[k, cc], yin.at[y], sent.at[2], y_recv, dev(hi_of[k] * 2 + c, x, cc)
+        ).start()
 
     stage_sum(0)
     stage_sum(1)
     stage_sum(2)
     stage_sum(3)
 
-    tell(1)
+    @pl.when(c == 1)
+    def _():
+        @pl.when(above)
+        def _():
+            pl.semaphore_wait(ready.at[2], 6)
+
+        @pl.when(jnp.logical_not(above))
+        def _():
+            pl.semaphore_wait(ready.at[2], 7)
+
+        signal(told.at[2], sibling)
 
     wait_for(state, state_sem)
     t = step_ref[0]
@@ -179,12 +244,36 @@
     first_fix = jnp.full((J, 128), 1.0 - p1, F32)
     second_fix = jnp.full((J, 128), 1.0 - p2, F32)
 
-    told_of(1)
+    @pl.when(c == 0)
+    def _():
+        pl.semaphore_wait(told.at[2], 1)
+
     stage_y(0)
     stage_y(1)
     stage_y(2)
     stage_y(3)
 
+    @pl.when(either(mate, above))
+    def _():
+        @pl.when(c == 1)
+        def _():
+            pl.semaphore_wait(ready.at[1], 1)
+            signal(told.at[1], sibling)
+
+        @pl.when(c == 0)
+        def _():
+            pl.semaphore_wait(told.at[1], 1)
+            for i, xx in enumerate((xo, xp, xm)):
+                @pl.when(both(mate, xx == 0))
+                def _(i=i, xx=xx):
+                    send_direct(3, i, xx)
+
+            for k in range(4):
+                @pl.when(both(above, hi_of[k] == 0))
+                def _(k=k):
+                    for cc in range(2):
+                        send_y(k, cc)
+
     def seven_or_eight(sem):
         @pl.when(c == ylo)
         def _():
@@ -194,9 +283,20 @@
         def _():
             wait_for(yin, sem)
 
+    @pl.when(x == 0)
+    def _():
+        wait_for(din.at[pl.ds(0, 3)], din_recv)
+        part[...] = decode(din[1]) + decode(din[2]) + decode(din[3])
+
     seven_or_eight(y_recv)
-    total = decode(yin[0])
-    for i in range(1, 8):
+
+    @pl.when(x != 0)
+    def _():
+        wait_for(din.at[0], din_recv)
+        part[...] = decode(din[0])
+
+    total = part[...]
+    for i in range(8):
         total = total + decode(yin[i])
 
     master = state[0]
@@ -324,9 +424,11 @@
             pltpu.VMEM((4, 3, 2, CODE, 128), I16),
             pltpu.VMEM((4, 2, CODE, 128), I16),
             pltpu.VMEM((8, CODE, 128), I16),
+            pltpu.VMEM((4, CODE, 128), I16),
+            pltpu.VMEM((J, 128), F32),
             pltpu.VMEM((3, J, 128), F32),
-            dma((4,)), dma, dma((4,)), dma((4,)), dma((4,)), dma, dma((18,)),
-            pltpu.SemaphoreType.REGULAR((2,)), pltpu.SemaphoreType.REGULAR((2,)),
+            dma((4,)), dma, dma((4,)), dma((4,)), dma((4,)), dma, dma, dma((18,)),
+            pltpu.SemaphoreType.REGULAR((4,)), pltpu.SemaphoreType.REGULAR((4,)),
         ],
         compiler_params=pltpu.CompilerParams(
             collective_id=0, has_side_effects=True, vmem_limit_bytes=24 << 20

time: 40.3 us -> 37.3 us (0.926)
  Pallas kernels: 38.9 us -> 35.8 us
    pallas_call x1, Pallas kernels: 37.7 us -> 34.6 us  [per_device(): pl.pallas_call(reduce_update_gather, out_shape=(row, row, row, jax.ShapeD...]
where the time goes in v6:
time: 37.3 us; the launch traced here: 37.1 us
  Pallas kernels  35.8 us (96%)
  between operations  1.29 us (3%)
    pallas_call x1, Pallas kernels, per_device(): pl.pallas_call(reduce_update_gather, out_shape=(row, row, row, jax.ShapeD...  34.6 us
    pallas_call x1, Pallas kernels, per_device(): pl.pallas_call(write_out, out_shape=(row, row, row, jax.ShapeDtypeStruct(...  1.22 us

profile of v6, /device:TPU:1, one launch (start us, length us, event | category | flops | bytes accessed | tf_op | source)
XLA Modules:
  0.0 37.1 jit_solution(10997809457754537184)
XLA Ops:
  1.3 34.6 %shard_map.84 = (f32[56,128]{1,0:T(8,128)S(1)}, f32[56,128]{1,0:T(8,128)S(1)}, f32[56,128]{1,0:T(8,128)S(1)}, bf16[64,56,128]{2,1,0:T(8,128)(2,1)S(1)}) custom-call(s32[1]{0:T(128)S(6)} %copy.9.step_ref, f32[8,56,8,128]{3,2,1,0:T(8,128)} %bitcast.9, f32[56,128]{1,0:T(8,128)} %bitcast.10, f32[56,128]{1,0:T(8,128)} %bitcast.11, f32[56,128]{1,0:T(8,128)} %bitcast.12), custom_call_target="tpu_custom_call" | custom-call | tf_op jit(solution)/shard_map/pallas_call | solution.py:414
  35.9 1.2 %shard_map.85 = (f32[56,128]{1,0:T(8,128)}, f32[56,128]{1,0:T(8,128)}, f32[56,128]{1,0:T(8,128)}, bf16[64,7168]{1,0:T(8,128)(2,1)}) custom-call(f32[56,128]{1,0:T(8,128)S(1)} %get-tuple-element.12.m_ref, f32[56,128]{1,0:T(8,128)S(1)} %get-tuple-element.13.v_ref, f32[56,128]{1,0:T(8,128)S(1)} %get-tuple-element.14.s_ref, ...), custom_call_target="tpu_custom_call" | custom-call | tf_op jit(solution)/shard_map/pallas_call | solution.py:440

commit v7 on v6

--- a/solution.py
+++ b/solution.py
@@ -34,8 +34,8 @@
 
 def reduce_update_gather(
     step_ref, g_ref, master_hbm, moment_hbm, second_hbm,
-    new_master_ref, new_moment_ref, new_second_ref, rows,
-    mine, sib, xs, xcode, xin, ycode, yin, din, part, state,
+    new_master_ref, new_moment_ref, new_second_ref, tiles,
+    rows, wide, mine, sib, xs, xcode, xin, ycode, yin, din, part, state,
     load_sem, state_sem, sent, d_recv, x_recv, y_recv, din_recv, a_recv, ready, told,
 ):
     ylo = lax.axis_index("pair")
@@ -376,32 +376,27 @@
     new_second_ref[...] = new_second
     arrived(32, SIBLING)
 
-    wait_for(sib, sent.at[0])
-    wait_for(xcode, sent.at[1])
-    seven_or_eight(sent.at[2])
-    wait_for(rows.at[pl.ds(0, 63)], sent.at[3])
-
-
-def write_out(
-    m_ref, v_ref, s_ref, rows, m_out, v_out, s_out, p_out, wide, tiles, sems, tile_sems,
-):
-    small = [
-        pltpu.make_async_copy(src, dst, sems.at[i])
-        for i, (src, dst) in enumerate(((m_ref, m_out), (v_ref, v_out), (s_ref, s_out)))
-    ]
-    for cp in small:
-        cp.start()
-    copies = []
     for gp in range(4):
         for s in range(16):
             wide[gp % 2, s] = rows[gp * 16 + s].astype(F32)
         w = wide.at[gp % 2].reshape(16 * J, 128)
         for j in range(J):
-            tiles[gp, :, pl.ds(j * 128, 128)] = w[pl.ds(j, 16, stride=J), :].astype(BF16)
-        cp = pltpu.make_async_copy(tiles.at[gp], p_out.at[pl.ds(gp * 16, 16), :], tile_sems.at[gp])
+            tiles[pl.ds(gp * 16, 16), pl.ds(j * 128, 128)] = w[pl.ds(j, 16, stride=J), :].astype(BF16)
+
+    wait_for(sib, sent.at[0])
+    wait_for(xcode, sent.at[1])
+    seven_or_eight(sent.at[2])
+    wait_for(rows.at[pl.ds(0, 63)], sent.at[3])
+
+
+def write_out(m_ref, v_ref, s_ref, p_ref, m_out, v_out, s_out, p_out, sems):
+    copies = [
+        pltpu.make_async_copy(src, dst, sems.at[i])
+        for i, (src, dst) in enumerate(((p_ref, p_out), (m_ref, m_out), (v_ref, v_out), (s_ref, s_out)))
+    ]
+    for cp in copies:
         cp.start()
-        copies.append(cp)
-    for cp in small + copies:
+    for cp in copies:
         cp.wait()
 
 
@@ -413,10 +408,12 @@
     dma = pltpu.SemaphoreType.DMA
     parts = pl.pallas_call(
         reduce_update_gather,
-        out_shape=(row, row, row, jax.ShapeDtypeStruct((64, J, 128), BF16)),
+        out_shape=(row, row, row, jax.ShapeDtypeStruct((64, J * 128), BF16)),
         in_specs=[pl.BlockSpec(memory_space=pltpu.SMEM)] + [hbm] * 4,
         out_specs=(vmem,) * 4,
         scratch_shapes=[
+            pltpu.VMEM((64, J, 128), BF16),
+            pltpu.VMEM((2, 16, J, 128), F32),
             pltpu.VMEM((4, J, 8, 128), F32),
             pltpu.VMEM((4, J, 8, 128), F32),
             pltpu.VMEM((4, 2, J, 128), F32),
@@ -443,9 +440,7 @@
         in_specs=[vmem] * 4,
         out_specs=(hbm,) * 4,
         scratch_shapes=[
-            pltpu.VMEM((2, 16, J, 128), F32),
-            pltpu.VMEM((4, 16, J * 128), BF16),
-            dma((3,)), dma((4,)),
+            dma((4,)),
         ],
         compiler_params=pltpu.CompilerParams(vmem_limit_bytes=24 << 20),
     )(*parts)

time: 37.3 us -> 37.5 us (level)
    pallas_call x1, Pallas kernels: 34.6 us -> 35.1 us  [per_device(): pl.pallas_call(reduce_update_gather, out_shape=(row, row, row, jax.ShapeD...]
where the time goes in v7:
time: 37.5 us; the launch traced here: 37.3 us
  Pallas kernels  36 us (96%)
  between operations  1.29 us (3%)
    pallas_call x1, Pallas kernels, per_device(): pl.pallas_call(reduce_update_gather, out_shape=(row, row, row, jax.ShapeD...  35.1 us
    pallas_call x1, Pallas kernels, per_device(): pl.pallas_call(write_out, out_shape=(row, row, row, jax.ShapeDtypeStruct(...  0.97 us

profile of v7, /device:TPU:1, one launch (start us, length us, event | category | flops | bytes accessed | tf_op | source)
XLA Modules:
  0.0 37.3 jit_solution(6093621146633143798)
XLA Ops:
  1.3 35.1 %shard_map.84 = (f32[56,128]{1,0:T(8,128)S(1)}, f32[56,128]{1,0:T(8,128)S(1)}, f32[56,128]{1,0:T(8,128)S(1)}, bf16[64,7168]{1,0:T(8,128)(2,1)S(1)}) custom-call(s32[1]{0:T(128)S(6)} %copy.9.step_ref, f32[8,56,8,128]{3,2,1,0:T(8,128)} %bitcast.9, f32[56,128]{1,0:T(8,128)} %bitcast.10, f32[56,128]{1,0:T(8,128)} %bitcast.11, f32[56,128]{1,0:T(8,128)} %bitcast.12), custom_call_target="tpu_custom_call" | custom-call | tf_op jit(solution)/shard_map/pallas_call | solution.py:409
  36.3 1.0 %shard_map.85 = (f32[56,128]{1,0:T(8,128)}, f32[56,128]{1,0:T(8,128)}, f32[56,128]{1,0:T(8,128)}, bf16[64,7168]{1,0:T(8,128)(2,1)}) custom-call(f32[56,128]{1,0:T(8,128)S(1)} %get-tuple-element.12.m_ref, f32[56,128]{1,0:T(8,128)S(1)} %get-tuple-element.13.v_ref, f32[56,128]{1,0:T(8,128)S(1)} %get-tuple-element.14.s_ref, ...), custom_call_target="tpu_custom_call" | custom-call | tf_op jit(solution)/shard_map/pallas_call | solution.py:437

commit v8 on v7

--- a/solution.py
+++ b/solution.py
@@ -14,7 +14,7 @@
 TOP = 32700.0
 STEPS = 256.0
 FAR = (1, 7, 2, 6, 3, 5, 4)
-Y_ORDER = (4, 3, 5, 1, 7, 2, 6)
+Y_ORDER = (1, 7, 4, 2, 6, 3, 5)
 A_ORDER = ("c1", "c7", "o", "c2", "c6", "c3", "c5", "c4", "b", "g1", "g7", "g2", "g6", "k", "g3", "g5", "g4")
 
 

time: 37.5 us -> 37.1 us (0.989)
  Pallas kernels: 36 us -> 35.6 us
    pallas_call x1, Pallas kernels: 35.1 us -> 34.6 us  [per_device(): pl.pallas_call(reduce_update_gather, out_shape=(row, row, row, jax.ShapeD...]
where the time goes in v8:
time: 37.1 us; the launch traced here: 36.9 us
  Pallas kernels  35.6 us (96%)
  between operations  1.29 us (3%)
    pallas_call x1, Pallas kernels, per_device(): pl.pallas_call(reduce_update_gather, out_shape=(row, row, row, jax.ShapeD...  34.6 us
    pallas_call x1, Pallas kernels, per_device(): pl.pallas_call(write_out, out_shape=(row, row, row, jax.ShapeDtypeStruct(...  0.97 us

profile of v8, /device:TPU:1, one launch (start us, length us, event | category | flops | bytes accessed | tf_op | source)
XLA Modules:
  0.0 36.9 jit_solution(6546550050299261746)
XLA Ops:
  1.3 34.6 %shard_map.84 = (f32[56,128]{1,0:T(8,128)S(1)}, f32[56,128]{1,0:T(8,128)S(1)}, f32[56,128]{1,0:T(8,128)S(1)}, bf16[64,7168]{1,0:T(8,128)(2,1)S(1)}) custom-call(s32[1]{0:T(128)S(6)} %copy.9.step_ref, f32[8,56,8,128]{3,2,1,0:T(8,128)} %bitcast.9, f32[56,128]{1,0:T(8,128)} %bitcast.10, f32[56,128]{1,0:T(8,128)} %bitcast.11, f32[56,128]{1,0:T(8,128)} %bitcast.12), custom_call_target="tpu_custom_call" | custom-call | tf_op jit(solution)/shard_map/pallas_call | solution.py:409
  35.9 1.0 %shard_map.85 = (f32[56,128]{1,0:T(8,128)}, f32[56,128]{1,0:T(8,128)}, f32[56,128]{1,0:T(8,128)}, bf16[64,7168]{1,0:T(8,128)(2,1)}) custom-call(f32[56,128]{1,0:T(8,128)S(1)} %get-tuple-element.12.m_ref, f32[56,128]{1,0:T(8,128)S(1)} %get-tuple-element.13.v_ref, f32[56,128]{1,0:T(8,128)S(1)} %get-tuple-element.14.s_ref, ...), custom_call_target="tpu_custom_call" | custom-call | tf_op jit(solution)/shard_map/pallas_call | solution.py:437
